TPU v7x, 256 devices: a whole 4x4x8 slice. The times are simulated.
256 devices in a mesh: dp: 64 (over x, y, z_hi), tensor: 4 (over z_lo, core).
Axes of the slice: x: 4, y: 4, z: 8 (z_hi: 4, z_lo: 2; z = z_hi * 2 + z_lo), core: 2. Of those that a mesh axis runs over, the one named last changes fastest.
Arguments:
- tokens: bfloat16 [32768, 6144], P('dp', 'tensor'), may hold values from -6 to 6
- block_mask: int32 [128, 4, 4], P('dp'), may hold values from 0 to 1
- norm_gain: float32 [6144], replicated, may hold values from 0.25 to 1.75
- w_query: bfloat16 [6144, 3072], P('dp', 'tensor'), may hold values from -0.078125 to 0.078125
- w_key: bfloat16 [6144, 3072], P('dp', 'tensor'), may hold values from -0.078125 to 0.078125
- w_value: bfloat16 [6144, 3072], P('dp', 'tensor'), may hold values from -0.078125 to 0.078125
- query_gain: float32 [128], replicated, may hold values from 0.1 to 1.9
- key_gain: float32 [128], replicated, may hold values from 0.1 to 1.9
Outputs:
- attended: bfloat16 [32768, 3072], P('dp', 'tensor')
All inputs are finite; a program needn't handle non-finite values.
Results may differ from a plain program's by a relative error of at most 0.0085.
Values may be sent and summed in bfloat16 or wider, within the bound.
A program may use at most 192 MiB of HBM per device.

v0:
```python
import jax
import jax.numpy as jnp
from jax import lax
from jax.sharding import PartitionSpec as P

DH = 128
TPD = 256
BLOCK = 64
EPS = 1e-06


def sent_together(arrays, axis, dim, along):
    widths = [a.shape[along] for a in arrays]
    both = jnp.concatenate(arrays, axis=along)
    whole = lax.all_gather(both, axis, axis=dim, tiled=True)
    return tuple(jnp.split(whole, [sum(widths[:k]) for k in range(1, len(widths))], axis=along))


def layer_norm(rows, gain):
    values = rows.astype(jnp.float32)
    mean = jnp.mean(values, axis=-1, keepdims=True)
    mean_sq = jnp.mean(values * values, axis=-1, keepdims=True)
    return (values - mean) * lax.rsqrt(mean_sq - mean * mean + EPS) * gain


def head_norm(values, gain):
    mean_sq = jnp.mean(values * values, axis=-1, keepdims=True)
    return values * lax.rsqrt(mean_sq + EPS) * gain


def add_rows(normed, piece):
    return jnp.dot(normed, piece, preferred_element_type=jnp.float32)


def per_device(tokens, block_mask, norm_gain, w_query, w_key, w_value, query_gain, key_gain):
    whole = lax.all_gather(tokens, "tensor", axis=1, tiled=True)
    normed = layer_norm(whole, norm_gain).astype(jnp.bfloat16)
    pieces = sent_together((w_query, w_key, w_value), "dp", 0, 1)
    query = add_rows(normed, pieces[0])
    key = add_rows(normed, pieces[1])
    value = add_rows(normed, pieces[2])
    draws_here = tokens.shape[0] // TPD
    heads_here = w_query.shape[1] // DH
    query_n = head_norm(query.reshape(draws_here, TPD, heads_here, DH), query_gain).astype(
        jnp.bfloat16
    )
    key_n = head_norm(key.reshape(draws_here, TPD, heads_here, DH), key_gain).astype(jnp.bfloat16)
    value = value.astype(jnp.bfloat16).reshape(draws_here, TPD, heads_here, DH)
    blocks = block_mask.shape[-1]
    allowed = (block_mask > 0) | (jnp.arange(blocks)[:, None] == jnp.arange(blocks)[None, :])[None]
    allowed = jnp.repeat(jnp.repeat(allowed, BLOCK, axis=1), BLOCK, axis=2)
    scores = jnp.einsum(
        "bqhe,bkhe->bhqk", query_n, key_n, preferred_element_type=jnp.float32
    ) / jnp.sqrt(jnp.float32(DH))
    scores = jnp.where(allowed[:, None], scores, jnp.float32(-1e30))
    top = jnp.max(scores, axis=-1, keepdims=True)
    weights = jnp.exp(scores - top)
    probs = (weights / jnp.sum(weights, axis=-1, keepdims=True)).astype(jnp.bfloat16)
    out = jnp.einsum("bhqk,bkhe->bqhe", probs, value, preferred_element_type=jnp.float32)
    return out.astype(jnp.bfloat16).reshape(tokens.shape[0], heads_here * DH)


def solution(mesh):
    return jax.shard_map(
        per_device,
        mesh=mesh,
        in_specs=(
            P("dp", "tensor"),
            P("dp", None, None),
            P(),
            P("dp", "tensor"),
            P("dp", "tensor"),
            P("dp", "tensor"),
            P(),
            P(),
        ),
        out_specs=P("dp", "tensor"),
        check_vma=False,
    )
```

profile of v0, /device:TPU:6, one launch (start us, length us, event | category | flops | bytes accessed | tf_op | source)
XLA Modules:
  0.0 385.1 jit_solution(3754338296619104776)
XLA Ops:
  6.5 0.0 copy-start.3
  6.5 0.0 all-gather.3.cloned.1.call-start
  6.5 0.7 all-gather.3.cloned.1.call-update
  7.3 0.0 all-gather.5.cloned.1.call-start
  7.3 1.8 pad_maximum_fusion
  9.2 0.0 all-gather.5.cloned.1.call-update
  9.2 0.7 compare_or_fusion
  9.9 0.1 copy.15
  10.0 0.1 broadcast_in_dim.14
  10.1 0.1 reshape.68
  10.2 67.4 %all-gather.3.cloned.1.call-done = bf16[512,6144]{1,0:T(8,128)(2,1)} async-done(((bf16[512,1536]{1,0:T(8,128)(2,1)}), bf16[512,6144]{1,0:T(8,128)(2,1)}) %all-gather.3.cloned.1.call-update) | async-done | bytes 6291472 | tf_op jit(solution)/shard_map/all_gather | solution.py:36
  77.6 4.8 %convert_reduce_fusion = (f32[512]{0:T(512)S(1)}, f32[512]{0:T(512)S(1)}) fusion(bf16[512,6144]{1,0:T(8,128)(2,1)} %all-gather.3.cloned.1.call-done), kind=kLoop, calls=%fused_computation.3 | loop fusion | flops 12581888 | bytes 6295552 | tf_op jit(solution)/shard_map/reduce_sum | solution.py:21
  82.4 249.8 %all-gather.5.cloned.1.call-done = bf16[6144,2304]{1,0:T(8,128)(2,1)} async-done(((bf16[96,2304]{1,0:T(8,128)(2,1)}), bf16[6144,2304]{1,0:T(8,128)(2,1)}) %all-gather.5.cloned.1.call-update) | async-done | bytes 28311568 | tf_op jit(solution)/shard_map/all_gather | solution.py:15
  332.2 0.0 copy-done.3
  332.2 10.9 %fusion.17 = bf16[512,768]{1,0:T(8,128)(2,1)S(1)} fusion(bf16[6144,2304]{1,0:T(8,128)(2,1)} %all-gather.5.cloned.1.call-done, bf16[512,6144]{1,0:T(8,128)(2,1)} %all-gather.3.cloned.1.call-done, f32[6144]{0:T(1024)S(1)} %copy-done.3, f32[512]{0:T(512)S(1)} %get-tuple-element.8, f32[512]{0:T(512)S(1)} %get-tuple-element.7), kind=kOutput, calls=%fused_computation.27 | convolution fusion | flops 4847960064 | bytes 16543744 | tf_op jit(solution)/shard_map/dot_general | solution.py:32
  343.1 1.9 reshape.72
  345.0 10.9 %fusion.7 = f32[512,768]{0,1:T(8,128)S(1)} fusion(bf16[6144,2304]{1,0:T(8,128)(2,1)} %all-gather.5.cloned.1.call-done, bf16[512,6144]{1,0:T(8,128)(2,1)} %all-gather.3.cloned.1.call-done, f32[6144]{0:T(1024)S(1)} %copy-done.3, f32[512]{0:T(512)S(1)} %get-tuple-element.8, f32[512]{0:T(512)S(1)} %get-tuple-element.7), kind=kOutput, calls=%fused_computation.10 | convolution fusion | flops 4847566848 | bytes 17330176 | tf_op jit(solution)/shard_map/dot_general | solution.py:32
  355.9 1.0 reshape.69
  356.9 12.0 %fusion.5 = f32[512,768]{0,1:T(8,128)} fusion(bf16[6144,2304]{1,0:T(8,128)(2,1)} %all-gather.5.cloned.1.call-done, bf16[512,6144]{1,0:T(8,128)(2,1)} %all-gather.3.cloned.1.call-done, f32[6144]{0:T(1024)S(1)} %copy-done.3, f32[512]{0:T(512)S(1)} %get-tuple-element.8, f32[512]{0:T(512)S(1)} %get-tuple-element.7), kind=kOutput, calls=%fused_computation.8 | convolution fusion | flops 4847566848 | bytes 17330176 | tf_op jit(solution)/shard_map/dot_general | solution.py:32
  369.0 0.0 copy-start.1
  369.0 0.0 copy-start.2
  369.0 2.3 reshape.70
  371.3 0.6 multiply_reduce_fusion
  371.9 0.6 multiply_reduce_fusion.1
  372.5 0.0 copy-done.1
  372.6 0.0 copy-done.2
  372.6 1.6 multiply_convert_fusion
  374.2 0.0 copy-start
  374.2 0.6 fusion.22
  374.9 1.1 fusion.30
  376.0 0.0 copy-done
  376.0 0.5 fusion.20
  376.5 0.8 copy.29
  377.3 1.0 copy.39
  (5 shorter events, 0.1 us)
Async XLA Ops:
  6.5 325.7 %copy-start.3 = (f32[6144]{0:T(1024)S(1)}, f32[6144]{0:T(1024)}, u32[]{:S(2)}) copy-start(f32[6144]{0:T(1024)} %param.10) | copy-start | bytes 73732
  6.5 71.1 %all-gather.3.cloned.1.call-start = ((), (), s32[]{:S(2)}) async-start(), calls=%async_computation | async-start | bytes 7864320 | tf_op jit(solution)/shard_map/all_gather | solution.py:36
  7.3 325.0 %all-gather.5.cloned.1.call-start = ((), (), s32[]{:S(2)}) async-start(), calls=%async_computation.1 | async-start | bytes 28753920 | tf_op jit(solution)/shard_map/all_gather | solution.py:15
  369.0 3.6 copy-start.1
  369.0 3.6 copy-start.2
  374.2 1.8 copy-start
Sparse Core Ops, SparseCore 0:
  9.1 68.4 all-gather.2
  80.9 251.3 all-gather.4
where the time goes:
time: 385 us
  waiting for transfers between devices  318 us (83%)
  matrix products  34.9 us (9%)
  between operations  13.5 us (4%)
  other arithmetic  11.4 us (3%)
  local copies, waits for them, and re-layouts  7.26 us (2%)
    all_gather x1, waiting for transfers between devices, sent_together(): whole = lax.all_gather(both, axis, axis=dim, tiled=True)  250 us
    all_gather x1, waiting for transfers between devices, per_device(): whole = lax.all_gather(tokens, 'tensor', axis=1, tiled=True)  67.4 us
    dot_general x3, matrix products, add_rows(): return jnp.dot(normed, piece, preferred_element_type=jnp.float32)  33.8 us
  transfers between devices with their start and end apart: 2, of which 2 were waited for; matrix products, arithmetic and copies ran while one was open for 2% of the time, Pallas kernels for 0%

commit v1 on v0

--- a/solution.py
+++ b/solution.py
@@ -33,7 +33,9 @@
 
 
 def per_device(tokens, block_mask, norm_gain, w_query, w_key, w_value, query_gain, key_gain):
-    whole = lax.all_gather(tokens, "tensor", axis=1, tiled=True)
+    whole = jnp.concatenate(
+        lax.all_to_all(jnp.stack(lax.psum(1, "tensor") * [tokens]), "tensor", 0, 0), axis=1
+    )
     normed = layer_norm(whole, norm_gain).astype(jnp.bfloat16)
     pieces = sent_together((w_query, w_key, w_value), "dp", 0, 1)
     query = add_rows(normed, pieces[0])

time: 385 us -> 373 us (0.969)
  waiting for transfers between devices: 318 us -> 224 us
  local copies, waits for them, and re-layouts: 7.26 us -> 82.3 us
  matrix products: 34.9 us -> 26.1 us
  other arithmetic: 11.4 us -> 18.8 us
  starting transfers between devices: 0.04 us -> 5.37 us
    all_gather x1, waiting for transfers between devices: 250 us -> 61.4 us  [sent_together(): whole = lax.all_gather(both, axis, axis=dim, tiled=True)]
    all_to_all x0 -> x1, waiting for transfers between devices: none -> 163 us  [per_device(): lax.all_to_all(jnp.stack(lax.psum(1, 'tensor') * [tokens]), 'tensor', 0, 0)]
    all_gather x1 -> x0, waiting for transfers between devices: 67.4 us -> none  [per_device(): whole = lax.all_gather(tokens, 'tensor', axis=1, tiled=True)]
    dot_general x0 -> x3, local copies, waits for them, and re-layouts: none -> 40.1 us  [add_rows(): return jnp.dot(normed, piece, preferred_element_type=jnp.float32)]
    convert_element_type x0 -> x2, local copies, waits for them, and re-layouts: none -> 25.9 us  [per_device(): normed = layer_norm(whole, norm_gain).astype(jnp.bfloat16)]
    convert_element_type x1 -> x2, other arithmetic: 1.64 us -> 11.2 us  [per_device(): normed = layer_norm(whole, norm_gain).astype(jnp.bfloat16)]
    dot_general x3, matrix products: 33.8 us -> 24.9 us  [add_rows(): return jnp.dot(normed, piece, preferred_element_type=jnp.float32)]
    all_to_all x0 -> x1, local copies, waits for them, and re-layouts: none -> 8.71 us  [per_device(): lax.all_to_all(jnp.stack(lax.psum(1, 'tensor') * [tokens]), 'tensor', 0, 0)]
  transfers between devices with their start and end apart: 2 -> 2, of which waited for: 2 -> 2; matrix products, arithmetic and copies ran while one was open for 2% -> 15% of each run, Pallas kernels for 0% -> 0%
where the time goes in v1:
time: 373 us; the launch traced here: 370 us
  waiting for transfers between devices  224 us (60%)
  local copies, waits for them, and re-layouts  82.3 us (22%)
  matrix products  26.1 us (7%)
  other arithmetic  18.8 us (5%)
  between operations  13.6 us (4%)
  starting transfers between devices  5.37 us (1%)
    all_to_all x1, waiting for transfers between devices, per_device(): lax.all_to_all(jnp.stack(lax.psum(1, 'tensor') * [tokens]), 'tensor', 0, 0)  163 us
    all_gather x1, waiting for transfers between devices, sent_together(): whole = lax.all_gather(both, axis, axis=dim, tiled=True)  61.4 us
    dot_general x3, local copies, waits for them, and re-layouts, add_rows(): return jnp.dot(normed, piece, preferred_element_type=jnp.float32)  40.1 us
    convert_element_type x2, local copies, waits for them, and re-layouts, per_device(): normed = layer_norm(whole, norm_gain).astype(jnp.bfloat16)  25.9 us
    dot_general x3, matrix products, add_rows(): return jnp.dot(normed, piece, preferred_element_type=jnp.float32)  24.9 us
    convert_element_type x2, other arithmetic, per_device(): normed = layer_norm(whole, norm_gain).astype(jnp.bfloat16)  11.2 us
    all_to_all x1, local copies, waits for them, and re-layouts, per_device(): lax.all_to_all(jnp.stack(lax.psum(1, 'tensor') * [tokens]), 'tensor', 0, 0)  8.71 us
  transfers between devices with their start and end apart: 2, of which 2 were waited for; matrix products, arithmetic and copies ran while one was open for 15% of the time, Pallas kernels for 0%

profile of v1, /device:TPU:6, one launch (start us, length us, event | category | flops | bytes accessed | tf_op | source)
XLA Modules:
  0.0 370.3 jit_solution(10217594063985905002)
XLA Ops:
  6.5 0.0 all-gather.2.cloned.1.call-start
  6.5 1.8 pad_maximum_fusion
  8.4 0.0 all-gather.2.cloned.1.call-update
  8.4 4.5 %stack.2 = bf16[4,512,1536]{2,1,0:T(8,128)(2,1)} broadcast(bf16[512,1536]{1,0:T(8,128)(2,1)} %param.8), dimensions={1,2} | broadcast | bytes 7864320 | tf_op jit(solution)/shard_map/stack | solution.py:37
  12.9 0.0 copy-start.3
  12.9 0.0 copy-start.2
  12.9 5.4 %all-to-all-start = ((bf16[4,512,1536]{2,1,0:T(8,128)(2,1)}), bf16[4,512,1536]{2,1,0:T(8,128)(2,1)}, u32[]{:S(2)}, u32[]{:S(2)}) async-start(bf16[4,512,1536]{2,1,0:T(8,128)(2,1)} %stack.2), calls=%async_computation | async-start | bytes 12582912 | tf_op jit(solution)/shard_map/all_to_all | solution.py:37
  18.3 0.0 copy-done.3
  18.3 0.1 copy.38
  18.5 0.1 broadcast_in_dim.14
  18.5 0.1 reshape.131
  18.6 0.0 copy-done.2
  18.6 162.7 %all-to-all-done = bf16[4,512,1536]{2,1,0:T(8,128)(2,1)} async-done(((bf16[4,512,1536]{2,1,0:T(8,128)(2,1)}), bf16[4,512,1536]{2,1,0:T(8,128)(2,1)}, u32[]{:S(2)}, u32[]{:S(2)}) %all-to-all-start) | async-done | bytes 6291488 | tf_op jit(solution)/shard_map/all_to_all | solution.py:37
  181.4 8.7 %copy.36 = bf16[4,512,1536]{1,2,0:T(8,128)(2,1)} copy(bf16[4,512,1536]{2,1,0:T(8,128)(2,1)} %all-to-all-done) | data formatting | bytes 12582912 | tf_op jit(solution)/shard_map/all_to_all | solution.py:37
  190.1 0.0 copy-start
  190.1 4.6 %convert_reduce_fusion = (f32[512]{0:T(512)S(1)}, f32[512]{0:T(512)S(1)}) fusion(bf16[4,512,1536]{1,2,0:T(8,128)(2,1)} %copy.36), kind=kLoop, calls=%fused_computation.11 | loop fusion | flops 12581888 | bytes 6295552 | tf_op jit(solution)/shard_map/reduce_sum | solution.py:21
  194.7 0.0 copy-done
  194.7 4.0 %fusion.6 = bf16[512,4,1536]{0,2,1:T(8,128)(2,1)} fusion(bf16[4,512,1536]{1,2,0:T(8,128)(2,1)S(1)} %copy-done, f32[4,1536]{1,0:T(4,128)S(1)} %mul.109, f32[512]{0:T(512)S(1)} %get-tuple-element.10, f32[512]{0:T(512)S(1)} %get-tuple-element.9), kind=kLoop, calls=%fused_computation.12 | loop fusion | flops 15728640 | bytes 12611584 | tf_op jit(solution)/shard_map/convert_element_type | solution.py:39
  198.7 9.7 %reshape.138 = bf16[2,256,6144]{1,0,2:T(2,128)(2,1)} reshape(bf16[512,4,1536]{0,2,1:T(8,128)(2,1)} %fusion.6) | data formatting | bytes 12582912 | tf_op jit(solution)/shard_map/convert_element_type | solution.py:39
  208.4 16.2 %copy.48 = bf16[2,256,6144,1]{2,1,3,0:T(8,128)(2,1)} copy(bf16[2,256,6144,1]{1,0,2,3:T(2,128)(2,1)} %bitcast.40) | data formatting | bytes 12582912 | tf_op jit(solution)/shard_map/convert_element_type | solution.py:39
  224.6 7.2 %fusion.3 = bf16[512,6144]{0,1:T(8,128)(2,1)} fusion(bf16[4,512,1536]{1,2,0:T(8,128)(2,1)} %copy.36, f32[6144]{0:T(1024)S(1)} %copy-done.2, f32[512]{0:T(512)S(1)} %get-tuple-element.10, f32[512]{0:T(512)S(1)} %get-tuple-element.9), kind=kLoop, calls=%fused_computation.4 | loop fusion | flops 15728640 | bytes 12611584 | tf_op jit(solution)/shard_map/convert_element_type | solution.py:39
  231.8 61.4 %all-gather.2.cloned.1.call-done = bf16[6144,2304]{1,0:T(8,128)(2,1)} async-done(((bf16[96,2304]{1,0:T(8,128)(2,1)}), bf16[6144,2304]{1,0:T(8,128)(2,1)}) %all-gather.2.cloned.1.call-update) | async-done | bytes 28311568 | tf_op jit(solution)/shard_map/all_gather | solution.py:15
  293.2 14.6 %slice_bitcast_fusion = (bf16[768,6144]{0,1:T(8,128)(2,1)}, bf16[768,6144]{0,1:T(8,128)(2,1)}) fusion(bf16[6144,2304]{1,0:T(8,128)(2,1)} %all-gather.2.cloned.1.call-done), kind=kLoop, calls=%fused_computation.7 | loop fusion | bytes 37748736 | tf_op jit(solution)/shard_map/dot_general | solution.py:32
  307.9 12.7 %copy.41 = bf16[768,6144]{1,0:T(8,128)(2,1)} copy(bf16[768,6144]{0,1:T(8,128)(2,1)} %get-tuple-element.7) | data formatting | bytes 18874368 | tf_op jit(solution)/shard_map/dot_general | solution.py:32
  320.5 9.9 %fusion.13 = bf16[512,768]{1,0:T(8,128)(2,1)S(1)} fusion(bf16[512,6144]{0,1:T(8,128)(2,1)} %fusion.3, bf16[6144,2304]{1,0:T(8,128)(2,1)} %all-gather.2.cloned.1.call-done), kind=kOutput, calls=%fused_computation.26 | convolution fusion | flops 4832231424 | bytes 16515072 | tf_op jit(solution)/shard_map/dot_general | solution.py:32
  330.5 0.9 reshape.137
  331.3 0.0 slice-start
  331.4 12.8 %copy.40 = bf16[768,6144]{1,0:T(8,128)(2,1)} copy(bf16[768,6144]{0,1:T(8,128)(2,1)} %get-tuple-element.8) | data formatting | bytes 18874368 | tf_op jit(solution)/shard_map/dot_general | solution.py:32
  344.2 0.0 copy-start.1
  344.2 0.0 slice-start.1
  344.2 9.9 %multiply_reduce_fusion.1 = (f32[2,256,6]{1,2,0:T(8,128)S(1)}, f32[2,256,6,128]{1,3,2,0:T(8,128)S(1)}) fusion(bf16[2,256,6144,1]{2,1,3,0:T(8,128)(2,1)} %copy.48, bf16[6,128,6144,1]{2,1,0,3:T(8,128)(2,1)} %bitcast.41), kind=kOutput, calls=%fused_computation.20 | convolution fusion | flops 4832621568 | bytes 17313792 | tf_op jit(solution)/shard_map/dot_general | solution.py:32
  354.1 0.0 slice-done
  354.1 0.0 copy-done.1
  354.1 0.0 slice-done.1
  354.1 0.0 copy-start.4
  354.1 0.0 copy-start.5
  354.1 5.1 %multiply_reduce_fusion.2 = (f32[2,256,6]{1,2,0:T(8,128)S(1)}, f32[2,256,6,128]{1,3,2,0:T(8,128)S(1)}) fusion(bf16[2,256,6144,1]{2,1,3,0:T(8,128)(2,1)S(1)} %bitcast.44, bf16[6,128,6144,1]{2,1,0,3:T(8,128)(2,1)S(1)} %bitcast.42), kind=kOutput, calls=%fused_computation.22 | convolution fusion | flops 4832621568 | bytes 17313792 | tf_op jit(solution)/shard_map/dot_general | solution.py:32
  359.2 0.0 copy-done.4
  359.3 0.0 copy-done.5
  359.3 0.7 fusion.17
  360.1 1.1 fusion.25
  361.2 0.5 fusion.16
  361.7 0.8 copy.57
  362.4 1.0 copy.63
  (7 shorter events, 0.1 us)
Async XLA Ops:
  6.5 286.7 %all-gather.2.cloned.1.call-start = ((), (), s32[]{:S(2)}) async-start(), calls=%async_computation.1 | async-start | bytes 28753920 | tf_op jit(solution)/shard_map/all_gather | solution.py:15
  12.9 5.4 %copy-start.3 = (s32[2,4,4]{2,1,0:T(4,128)S(1)}, s32[2,4,4]{2,1,0:T(4,128)}, u32[]{:S(2)}) copy-start(s32[2,4,4]{2,1,0:T(4,128)} %param.9) | copy-start | bytes 388
  12.9 5.7 %copy-start.2 = (f32[6144]{0:T(1024)S(1)}, f32[6144]{0:T(1024)}, u32[]{:S(2)}) copy-start(f32[6144]{0:T(1024)} %param.10) | copy-start | bytes 73732
  12.9 168.4 %all-to-all-start = ((bf16[4,512,1536]{2,1,0:T(8,128)(2,1)}), bf16[4,512,1536]{2,1,0:T(8,128)(2,1)}, u32[]{:S(2)}, u32[]{:S(2)}) async-start(bf16[4,512,1536]{2,1,0:T(8,128)(2,1)} %stack.2), calls=%async_computation | async-start | bytes 12582912 | tf_op jit(solution)/shard_map/all_to_all | solution.py:37
  190.1 4.6 %copy-start = (bf16[4,512,1536]{1,2,0:T(8,128)(2,1)S(1)}, bf16[4,512,1536]{1,2,0:T(8,128)(2,1)}, u32[]{:S(2)}) copy-start(bf16[4,512,1536]{1,2,0:T(8,128)(2,1)} %copy.36) | copy-start | bytes 18874372
  331.3 22.7 %slice-start = ((s8[6291456]{0:T(1024)(128)(4,1)}), s8[2097152]{0:T(1024)(128)(4,1)S(1)}, s32[]{:S(2)}) async-start(s8[6291456]{0:T(1024)(128)(4,1)} %bitcast.43), calls=%async_computation.2 | async-start | bytes 4194304
  344.2 9.9 %copy-start.1 = (bf16[768,6144]{1,0:T(8,128)(2,1)S(1)}, bf16[768,6144]{1,0:T(8,128)(2,1)}, u32[]{:S(2)}) copy-start(bf16[768,6144]{1,0:T(8,128)(2,1)} %copy.40) | copy-start | bytes 28311556
  344.2 9.9 %slice-start.1 = ((s8[6291456]{0:T(1024)(128)(4,1)}), s8[4194304]{0:T(1024)(128)(4,1)S(1)}, s32[]{:S(2)}) async-start(s8[6291456]{0:T(1024)(128)(4,1)} %bitcast.43), calls=%async_computation.3 | async-start | bytes 8388608
  354.1 5.1 %copy-start.4 = (f32[128]{0:T(128)S(1)}, f32[128]{0:T(128)}, u32[]{:S(2)}) copy-start(f32[128]{0:T(128)} %param.15) | copy-start | bytes 1540
  354.1 5.1 %copy-start.5 = (f32[128]{0:T(128)S(1)}, f32[128]{0:T(128)}, u32[]{:S(2)}) copy-start(f32[128]{0:T(128)} %param.14) | copy-start | bytes 1540
Sparse Core Ops, SparseCore 0:
  10.6 282.5 all-gather.1
